TPU v7x, 256 devices: a whole 4x4x8 slice. The times are simulated.
256 devices in a mesh: track: 16 (over z, x_lo), tm: 16 (over x_hi, y, core).
Axes of the slice: x: 4 (x_hi: 2, x_lo: 2; x = x_hi * 2 + x_lo), y: 4, z: 8, core: 2. Of those that a mesh axis runs over, the one named last changes fastest.
Arguments:
- positions: float32 [3, 32, 6144], P(None, 'tm', 'track'), may hold values from -6 to 6
- embeddings: float32 [32, 128, 6144], P('tm', None, 'track'), may hold values from -6 to 6
- visible: int32 [32, 6144], P('tm', 'track'), may hold values 0 or 1
Outputs:
- grad_positions: float32 [3, 32, 6144], P(None, 'tm', 'track')
- grad_embeddings: float32 [32, 128, 6144], P('tm', None, 'track')
- mean_loss: float32 [], replicated
All inputs are finite; a program needn't handle non-finite values. No bound on the sum of `visible` on one device may be relied on, other than what follows from the above.
Results may differ from a plain program's by a relative error of at most 0.00014.
Values sent between devices are 32-bit elements; how exact they have to be, the bound alone decides.
A program may use at most 128 MiB of HBM per device.

v0:
```python
import math

import jax
import jax.numpy as jnp
from jax import lax
from jax.sharding import PartitionSpec as P

rigidity = 4.0
highest = lax.Precision.HIGHEST


def shifted(array, axis, by):
    size = lax.axis_size(axis)
    pairs = [(i, i + by) for i in range(size) if 0 <= i + by < size]
    return lax.ppermute(array, axis, pairs)


def tile_terms(pos_a, mask_a, emb_a, pos_b, mask_b, emb_b, weight_scale):
    inv_root = 1.0 / math.sqrt(emb_a.shape[1])
    offset = pos_a[:, :, :, None] - pos_b[:, :, None, :]
    distance = jnp.sqrt(jnp.sum(offset * offset, axis=0) + 1.0)
    change = distance[1:] - distance[:-1]
    both_seen = mask_a[:, :, None] * mask_b[:, None, :]
    seen_pair = both_seen[1:] * both_seen[:-1]
    logits = jnp.einsum("fei,fej->fij", emb_a, emb_b, precision=highest) * inv_root
    affinity = jax.nn.sigmoid(logits)
    squared = seen_pair * change * change
    energy = jnp.sum(affinity * squared)
    grad_change = 2.0 * weight_scale * affinity * seen_pair * change
    padding = jnp.zeros_like(grad_change[:1])
    grad_dist = jnp.concatenate([padding, grad_change], 0) - jnp.concatenate(
        [grad_change, padding], 0
    )
    scaled = (grad_dist / distance)[None] * offset
    grad_pos_a = jnp.sum(scaled, axis=3)
    grad_pos_b = -jnp.sum(scaled, axis=2)
    grad_logit = weight_scale * squared * affinity * (1.0 - affinity) * inv_root
    grad_emb_a = jnp.einsum("fij,fej->fei", grad_logit, emb_b, precision=highest)
    grad_emb_b = jnp.einsum("fij,fei->fej", grad_logit, emb_a, precision=highest)
    return (energy, grad_pos_a, grad_emb_a, grad_pos_b, grad_emb_b)


def on_device(positions, embeddings, visible):
    frames_local = embeddings.shape[0]
    block_width = embeddings.shape[2]
    tracks = block_width * lax.axis_size("track")
    frames = frames_local * lax.axis_size("tm")
    weight_scale = rigidity / math.sqrt(tracks)
    seen_mask = visible.astype(jnp.float32)
    next_pos, next_mask = shifted((positions[:, :1], seen_mask[:1]), "tm", -1)
    pos_ext = jnp.concatenate([positions, next_pos], 1)
    mask_ext = jnp.concatenate([seen_mask, next_mask], 0)
    packed = jnp.concatenate([pos_ext, mask_ext[None]], 0)

    def own_tile(others_packed, others_emb):
        return tile_terms(
            pos_ext,
            mask_ext,
            embeddings,
            others_packed[:3],
            others_packed[3],
            others_emb,
            weight_scale,
        )

    initial = (jnp.zeros_like(pos_ext), jnp.zeros_like(embeddings), jnp.zeros((), jnp.float32))
    piece_packed = lax.all_gather(packed, "track", axis=2, tiled=True)
    piece_emb = lax.all_gather(embeddings, "track", axis=2, tiled=True)
    columns = piece_emb.shape[2]
    blocks = columns // block_width
    split_packed = jnp.moveaxis(
        piece_packed.reshape(4, frames_local + 1, blocks, block_width), 2, 0
    )
    split_emb = jnp.moveaxis(
        piece_emb.reshape(frames_local, piece_emb.shape[1], blocks, block_width), 2, 0
    )

    def advance(inner, others):
        energy, grad_pos_a, grad_emb_a, unused_pos, unused_emb = own_tile(others[0], others[1])
        return ((inner[0] + grad_pos_a, inner[1] + grad_emb_a, inner[2] + energy), None)

    result, unused = lax.scan(advance, initial, (split_packed, split_emb))
    grad_pos, grad_emb, energy_sum = result
    energy_sum = 0.5 * energy_sum
    incoming = shifted(grad_pos[:, -1:], "tm", 1)
    grad_positions = grad_pos[:, :-1]
    grad_positions = jnp.concatenate([grad_positions[:, :1] + incoming, grad_positions[:, 1:]], 1)
    total = lax.psum(energy_sum, ("track", "tm"))
    mean_loss = total / (tracks * (tracks - 1) / 2.0 * (frames - 1))
    return (grad_positions, grad_emb, mean_loss)


def solution(mesh):
    in_specs = (P(None, "tm", "track"), P("tm", None, "track"), P("tm", "track"))
    out_specs = (P(None, "tm", "track"), P("tm", None, "track"), P())
    return jax.shard_map(
        on_device, mesh=mesh, in_specs=in_specs, out_specs=out_specs, check_vma=False
    )
```

profile of v0, /device:TPU:6, one launch (start us, length us, event | category | flops | bytes accessed | tf_op | source)
XLA Modules:
  0.0 580.2 jit_solution(791380038999158030)
XLA Ops:
  7.2 1.9 copy.30
  9.9 5.2 collective-permute-start
  15.8 2.6 collective-permute-start.1
  20.4 47.5 %all_gather.7 = f32[4,3,6144]{2,1,0:T(4,128)S(1)} all-gather(f32[4,3,384]{2,1,0:T(4,128)S(1)} %pad_maximum_fusion), channel_id=1, replica_groups=mesh['track'=16,'tm'=16] {'track'}, dimensions={2}, use_global_device_ids=true | all-gather | bytes 313344 | tf_op jit(solution)/shard_map/all_gather | solution.py:67
  69.5 90.6 %all-gather.2.cloned.1.call-done = f32[2,128,6144]{1,2,0:T(8,128)} async-done(((f32[2,128,384]{1,2,0:T(8,128)}), f32[2,128,6144]{1,2,0:T(8,128)}) %all-gather.2.cloned.1.call-update) | async-done | bytes 6291472 | tf_op jit(solution)/shard_map/all_gather | solution.py:68
  160.0 327.7 %while.15 = (s32[]{:T(128)}, f32[3,3,384]{2,1,0:T(4,128)}, f32[2,128,384]{2,1,0:T(8,128)}, f32[]{:T(128)}, f32[16,2,128,384]{2,3,0,1:T(8,128)}, /*index=5*/f32[2...) while((s32[]{:T(128)}, f32[3,3,384]{2,1,0:T(4,128)}, ...), condition=%wide.region_4.5_spmd.clone, body=%wide.region_0.4_spmd.clone.sunk | while | flops 922389888 | bytes 49315164 | solution.py:82
  162.4 1.6 fusion.34
  166.1 5.0 multiply_reduce_fusion.2
  171.9 4.3 convolution_add_fusion.2
  178.0 1.8 fusion.35
  182.8 1.6 fusion.34
  186.5 5.0 multiply_reduce_fusion.2
  192.3 4.4 convolution_add_fusion.2
  198.5 1.8 fusion.35
  203.3 1.6 fusion.34
  207.0 5.0 multiply_reduce_fusion.2
  212.7 4.4 convolution_add_fusion.2
  219.0 1.8 fusion.35
  223.7 1.6 fusion.34
  227.5 5.0 multiply_reduce_fusion.2
  233.2 4.4 convolution_add_fusion.2
  239.5 1.8 fusion.35
  244.2 1.6 fusion.34
  248.0 5.0 multiply_reduce_fusion.2
  253.7 4.4 convolution_add_fusion.2
  260.0 1.8 fusion.35
  264.7 1.6 fusion.34
  268.5 5.0 multiply_reduce_fusion.2
  274.2 4.4 convolution_add_fusion.2
  280.5 1.8 fusion.35
  285.2 1.6 fusion.34
  289.0 5.0 multiply_reduce_fusion.2
  294.7 4.4 convolution_add_fusion.2
  300.9 1.8 fusion.35
  305.7 1.6 fusion.34
  309.4 5.0 multiply_reduce_fusion.2
  315.2 4.4 convolution_add_fusion.2
  321.4 1.8 fusion.35
  329.9 5.0 multiply_reduce_fusion.2
  335.7 4.4 convolution_add_fusion.2
  341.9 1.8 fusion.35
  350.4 5.0 multiply_reduce_fusion.2
  356.2 4.4 convolution_add_fusion.2
  362.4 1.8 fusion.35
  370.9 5.0 multiply_reduce_fusion.2
  376.6 4.4 convolution_add_fusion.2
  382.9 1.8 fusion.35
  391.4 5.0 multiply_reduce_fusion.2
  397.1 4.4 convolution_add_fusion.2
  403.4 1.8 fusion.35
  411.9 5.0 multiply_reduce_fusion.2
  417.6 4.4 convolution_add_fusion.2
  423.9 1.8 fusion.35
  432.4 5.0 multiply_reduce_fusion.2
  438.1 4.4 convolution_add_fusion.2
  444.3 1.8 fusion.35
  452.9 5.0 multiply_reduce_fusion.2
  458.6 4.4 convolution_add_fusion.2
  464.8 1.8 fusion.35
  473.3 5.0 multiply_reduce_fusion.2
  479.1 4.4 convolution_add_fusion.2
  485.3 1.8 fusion.35
  488.5 1.9 collective-permute-start.2
  490.4 79.7 %psum.7 = f32[]{:T(128)} all-reduce(f32[]{:T(128)S(6)} %mul_shard_map.3), channel_id=1, replica_groups=mesh['track'=16,'tm'=16] {'track','tm'}, use_global_device_ids=true, to_apply=%region_5.6 | all-reduce | flops 1 | bytes 8 | tf_op jit(solution)/shard_map/psum | solution.py:88
  (363 shorter events, 129.8 us)
Async XLA Ops:
  7.2 61.7 %copy-start.6 = (f32[3,2,384]{2,1,0:T(2,128)S(1)}, f32[3,2,384]{2,1,0:T(2,128)}, u32[]{:S(2)}) copy-start(f32[3,2,384]{2,1,0:T(2,128)} %param.5) | copy-start | bytes 27652
  7.2 152.9 %all-gather.2.cloned.1.call-start = ((), (), s32[]{:S(2)}) async-start(), calls=%async_computation | async-start | bytes 6684672 | tf_op jit(solution)/shard_map/all_gather | solution.py:68
  9.9 8.5 %collective-permute-start = (f32[1,384]{1,0:T(1,128)S(1)}, f32[1,384]{1,0:T(1,128)S(1)}, u32[]{:S(2)}, u32[]{:S(2)}) collective-permute-start(f32[1,384]{1,0:T(1,128)S(1)} %slice.53), channel_id=1, source_target_pairs={{1,0},{2,1},{3,2},{4,3},{5,4},{6,5},{7,6},{8,7},{9,8},{10,9},{11,1... | collective-permute-start | bytes 4616 | tf_op jit(solution)/shard_map/ppermute | solution.py:15
  15.8 3.9 collective-permute-start.1
  165.1 1.0 copy-start.5
  165.8 5.4 copy-start
  171.8 4.3 copy-start.1
  178.0 1.8 copy-start.3
  185.5 1.0 copy-start.5
  186.2 5.4 copy-start
  192.3 4.4 copy-start.1
  198.5 1.8 copy-start.3
  206.0 1.0 copy-start.5
  206.7 5.4 copy-start
  212.7 4.4 copy-start.1
  219.0 1.8 copy-start.3
  226.5 1.0 copy-start.5
  227.1 5.4 copy-start
  233.2 4.4 copy-start.1
  239.5 1.8 copy-start.3
  247.0 1.0 copy-start.5
  247.6 5.4 copy-start
  253.7 4.4 copy-start.1
  260.0 1.8 copy-start.3
  267.5 1.0 copy-start.5
  268.1 5.4 copy-start
  274.2 4.4 copy-start.1
  280.4 1.8 copy-start.3
  288.0 1.0 copy-start.5
  288.6 5.4 copy-start
  294.7 4.4 copy-start.1
  300.9 1.8 copy-start.3
  308.4 1.0 copy-start.5
  309.1 5.4 copy-start
  315.2 4.4 copy-start.1
  321.4 1.8 copy-start.3
  328.9 1.0 copy-start.5
  329.6 5.4 copy-start
  335.7 4.4 copy-start.1
  341.9 1.8 copy-start.3
  349.4 1.0 copy-start.5
  350.1 5.4 copy-start
  356.1 4.4 copy-start.1
  362.4 1.8 copy-start.3
  369.9 1.0 copy-start.5
  370.6 5.4 copy-start
  376.6 4.4 copy-start.1
  382.9 1.8 copy-start.3
  391.0 5.4 copy-start
  397.1 4.4 copy-start.1
  403.4 1.8 copy-start.3
  411.5 5.4 copy-start
  417.6 4.4 copy-start.1
  423.8 1.8 copy-start.3
  432.0 5.4 copy-start
  438.1 4.4 copy-start.1
  444.3 1.8 copy-start.3
  452.5 5.4 copy-start
  458.6 4.4 copy-start.1
  464.8 1.8 copy-start.3
  473.0 5.4 copy-start
  479.1 4.4 copy-start.1
  485.3 1.8 copy-start.3
  488.5 82.3 %collective-permute-start.2 = (f32[3,1,384]{2,1,0:T(1,128)S(1)}, f32[3,1,384]{2,1,0:T(1,128)S(1)}, u32[]{:S(2)}, u32[]{:S(2)}) collective-permute-start(f32[3,1,384]{2,1,0:T(1,128)S(1)} %slice.41), channel_id=1, source_target_pairs={{0,1},{1,2},{2,3},{3,4},{4,5},{5,6},{6,7},{7,8},{8,9},{9,10},{10,1... | collective-permute-start | bytes 13832 | tf_op jit(solution)/shard_map/ppermute | solution.py:15
  (37 other events, 24.3 us)
Sparse Core Ops, SparseCore 0:
  9.8 150.2 all-gather.1
where the time goes:
time: 586 us; the launch traced here: 580 us
  matrix products  151 us (26%)
  blocking collectives  127 us (22%)
  local copies, waits for them, and re-layouts  94.3 us (16%)
  waiting for transfers between devices  91.9 us (16%)
  other arithmetic  77.4 us (13%)
  between operations  15.9 us (3%)
  loops' own time  12.7 us (2%)
  starting transfers between devices  9.71 us (2%)
    all_gather x1, waiting for transfers between devices, on_device(): piece_emb = lax.all_gather(embeddings, 'track', axis=2, tiled=True)  90.6 us
    dot_general x16, matrix products, tile_terms(): jnp.einsum('fei,fej->fij', emb_a, emb_b, precision=highest) * inv_root  80.6 us
    psum x1, blocking collectives, on_device(): total = lax.psum(energy_sum, ('track', 'tm'))  79.7 us
    dot_general x16, matrix products, tile_terms(): jnp.einsum('fij,fej->fei', grad_logit, emb_b, precision=highest)  70.5 us
    all_gather x1, blocking collectives, on_device(): piece_packed = lax.all_gather(packed, 'track', axis=2, tiled=True)  47.5 us
    reduce_sum x16, other arithmetic, tile_terms(): grad_pos_a = jnp.sum(scaled, axis=3)  28.8 us
    while x224, local copies, waits for them, and re-layouts  24.9 us
    reduce_sum x16, other arithmetic, tile_terms(): distance = jnp.sqrt(jnp.sum(offset * offset, axis=0) + 1.0)  24.9 us
  transfers between devices with their start and end apart: 4, of which 2 were waited for; matrix products, arithmetic and copies ran while one was open for 1% of the time, Pallas kernels for 0%

commit v1 on v0

v1 whole, which is shorter than its diff:
```python
import functools
import math

import jax
import jax.numpy as jnp
from jax import lax
from jax.experimental import pallas as pl
from jax.experimental.pallas import tpu as pltpu
from jax.sharding import PartitionSpec as P

f32, bf16 = jnp.float32, jnp.bfloat16
MESH = pl.DeviceIdType.MESH
rigidity = 4.0
HIDE = 2.0**20
LANE = 128
NBUF = 2

ROWS = 8
PLANES = 8
STEPS = 4


def owner(z, f):
    rel = lax.rem(z - 2 * f + 2 * ROWS, ROWS)
    upper = jnp.where((rel >= 1) & (rel <= 4), 1, 0)
    away = jnp.where(upper == 1, rel - 1, lax.rem(ROWS - rel, ROWS))
    other = jnp.where((away == 1) | (away == 2), 1, 0)
    slot = jnp.where(away >= 2, 1, 0)
    return 2 * f + upper, slot, other


def flip(core, other):
    return core + other - 2 * core * other


def split2(v):
    hi = v.astype(bf16)
    return hi, (v - hi.astype(f32)).astype(bf16)


def pieces(v):
    h = v.astype(bf16).astype(f32)
    m = (v - h).astype(bf16).astype(f32)
    return h, m, (v - h - m).astype(bf16).astype(f32)


def prep_cols(u, emb, width, buf, pc, mid, rhs, rd):
    for s in range(2):
        cs = slice(s * width, (s + 1) * width)
        hi, lo = split2(buf[u, s, 0:emb, :])
        rhs[u, 0:emb, cs] = hi
        rhs[u, emb : 2 * emb, cs] = lo
        rhs[u, 2 * emb : 3 * emb, cs] = hi
        q = buf[u, s, emb + 3 : emb + 4, :] * buf[u, s, emb + 11 : emb + 12, :]
        rows = lax.broadcasted_iota(jnp.int32, (LANE, width), 0)
        m = jnp.where(rows == 0, 1.0, 0.0) + jnp.where(rows == 1, (q - 1.0) * HIDE, 0.0)
        rhs[u, 3 * emb :, cs] = m.astype(bf16)
        for f in range(2):
            p = [
                buf[u, s, emb + 8 * f + c : emb + 8 * f + c + 1, :] - mid[8 * f + c : 8 * f + c + 1, 0:1]
                for c in range(3)
            ]
            out = []
            for c in range(3):
                pc[u, s, 8 * f + c : 8 * f + c + 1, :] = p[c]
                h, mm, l = pieces(p[c])
                out += [h, mm, h, mm, l, h]
            n = p[0] * p[0] + p[1] * p[1] + p[2] * p[2]
            one = jnp.ones_like(n)
            out += [one, one, one] + list(pieces(n)) + [jnp.zeros((8, width), f32)]
            rd[u, f, :, cs] = jnp.concatenate(out, 0).astype(bf16)


def prep_rows(valid, emb, width, buf, mid, ll, ld, tp):
    mean = (jnp.sum(buf[0, 0, emb:, :], 1, keepdims=True) + jnp.sum(buf[0, 1, emb:, :], 1, keepdims=True)) / (2.0 * width)
    mid[...] = jnp.broadcast_to(mean, mid.shape)
    for s in range(2):
        rs = slice(s * width, (s + 1) * width)
        hi, lo = split2(jnp.transpose(buf[0, s, 0:emb, :]) * (0.5 / math.sqrt(emb)))
        ll[rs, 0:emb] = hi
        ll[rs, emb : 2 * emb] = hi
        ll[rs, 2 * emb : 3 * emb] = lo
        q = buf[0, s, emb + 3 : emb + 4, :] * buf[0, s, emb + 11 : emb + 12, :] * valid
        one = jnp.ones_like(q)
        m = jnp.concatenate([(q - 1.0) * HIDE, one, jnp.zeros((LANE - 2, width), f32)], 0)
        ll[rs, 3 * emb :] = jnp.transpose(m).astype(bf16)
        for f in range(2):
            p = [
                buf[0, s, emb + 8 * f + c : emb + 8 * f + c + 1, :] - mid[8 * f + c : 8 * f + c + 1, 0:1]
                for c in range(3)
            ]
            out = []
            for c in range(3):
                h, mm, l = pieces(p[c])
                out += [-2.0 * h, -2.0 * h, -2.0 * mm, -2.0 * mm, -2.0 * h, -2.0 * l]
            n = p[0] * p[0] + p[1] * p[1] + p[2] * p[2] + 1.0
            out += list(pieces(n)) + [one, one, one, jnp.zeros((LANE - 24, width), f32)]
            ld[f, rs, :] = jnp.transpose(jnp.concatenate(out, 0)).astype(bf16)[:, 0:32]
            tp[f, rs, :] = jnp.transpose(jnp.concatenate(p + [jnp.zeros((LANE - 3, width), f32)], 0))


def dot_piece(k, n, u, r0, R, rhs, rd, ll, ld, sc):
    ns = slice(n, n + 256)
    if k == 0:
        sc[0][:, ns] = jnp.dot(ll[r0 : r0 + R, :], rhs[u, :, ns], preferred_element_type=f32)
    else:
        sc[k][:, ns] = jnp.dot(ld[k - 1, r0 : r0 + R, :], rd[u, k - 1, :, ns], preferred_element_type=f32)


def strip(s, u, r0, R, width, pc, acc, en, sc):
    xs, d0s, d1s, gs = sc
    A = [acc[k, r0 + s : r0 + s + 16, :] for k in range(8)]
    es = en[...]
    span = 256
    for c0 in range(0, 2 * width, span):
        cs = slice(c0, c0 + span)
        x, a0, a1 = xs[s : s + 16, cs], d0s[s : s + 16, cs], d1s[s : s + 16, cs]
        q0, q1 = lax.rsqrt(a0), lax.rsqrt(a1)
        ch = a1 * q1 - a0 * q0
        v = jnp.tanh(x) * ch
        h = ch + v
        g = h * (ch - v)
        hi = g.astype(bf16)
        gs[s : s + 16, cs] = hi
        gs[R + s : R + s + 16, cs] = (g - hi.astype(f32)).astype(bf16)
        e = h * ch
        w = (h * q0, h * q1)
        for k in range(0, span, LANE):
            j = c0 + k
            side, js = j // width, slice(j % width, j % width + LANE)
            for f in range(2):
                wk = w[f][:, k : k + LANE]
                A[4 * f] = A[4 * f] + wk
                for c in range(3):
                    A[4 * f + 1 + c] = A[4 * f + 1 + c] + wk * pc[u, side, 8 * f + c : 8 * f + c + 1, js]
            es = es + (e[0:8, k : k + LANE] + e[8:16, k : k + LANE])
    for k in range(8):
        acc[k, r0 + s : r0 + s + 16, :] = A[k]
    en[...] = es


def grad_dot(u, r0, R, emb, rhs, ge, sc):
    o = lax.dot_general(
        sc[3][...], rhs[u, 0 : 2 * emb, :], (((1,), (1,)), ((), ())), preferred_element_type=f32
    )
    ge[r0 : r0 + R, :] = ge[r0 : r0 + R, :] + ((o[:R, :emb] + o[:R, emb:]) + o[R:, :emb])


def unit(u, R, emb, width, pc, rhs, rd, ll, ld, scs, acc, ge, en):
    todo = [(k, n) for n in range(0, 2 * width, 256) for k in range(3)]
    chunks = list(range(0, 2 * width, R))
    strips = list(range(0, R, 16))
    per = -(-len(todo) // len(strips))
    for k, n in todo:
        dot_piece(k, n, u, chunks[0], R, rhs, rd, ll, ld, scs[0])
    for i, r0 in enumerate(chunks):
        later = list(todo) if i + 1 < len(chunks) else []
        for j, s in enumerate(strips):
            strip(s, u, r0, R, width, pc, acc, en, scs[i % NBUF])
            if j == 0 and i > 0:
                grad_dot(u, chunks[i - 1], R, emb, rhs, ge, scs[(i - 1) % NBUF])
            for _ in range(per):
                if later:
                    k, n = later.pop(0)
                    dot_piece(k, n, u, chunks[i + 1], R, rhs, rd, ll, ld, scs[(i + 1) % NBUF])
    grad_dot(u, chunks[-1], R, emb, rhs, ge, scs[(len(chunks) - 1) % NBUF])


def finish(weight, emb, width, acc, ge, tp, gres, pres):
    for s in range(2):
        rs = slice(s * width, (s + 1) * width)
        gres[s] = jnp.transpose(ge[rs, :]) * (weight / (4.0 * math.sqrt(emb)))
        cols = lax.broadcasted_iota(jnp.int32, (width, LANE), 1)
        for f in range(2):
            ss = jnp.sum(acc[4 * f, rs, :], axis=1, keepdims=True)
            tt = jnp.zeros((width, LANE), f32)
            for c in range(3):
                tc = jnp.sum(acc[4 * f + 1 + c, rs, :], axis=1, keepdims=True)
                tt = tt + jnp.where(cols == c, tc, 0.0)
            res = (ss * tp[f, rs, :] - tt) * (weight if f else -weight)
            pres[s, f] = jnp.transpose(res)[0:8, :]


def kernel(
    R, emb, width, tracks, frames,
    e_ref, pm_ref, gemb, gpos, lout,
    buf, pc, mid, rhs, rd, ll, ld, tp, acc, ge, en, gres, pres, prec, l1, l2,
    *rest,
):
    scs = [rest[4 * i : 4 * i + 4] for i in range(NBUF)]
    r1, s1, rg, sg, rr, sr, rl, sl = rest[4 * NBUF :]
    weight = rigidity / math.sqrt(tracks)
    n_track, n_tm = 16, 16
    track, tm = lax.axis_index("track"), lax.axis_index("tm")
    z, xl = track // 2, lax.rem(track, 2)
    plane, core = tm // 2, lax.rem(tm, 2)
    step = z // 2

    cur_to, next_to = [], []
    for l in range(2):
        f = 2 * core + l
        dz, slot, other = owner(z, f)
        cur_to.append((2 * dz + xl, 2 * plane + flip(core, other), slot))
        s = lax.rem(f + STEPS - 1, STEPS)
        back = jnp.where(f == 0, 1, 0)
        dz, slot, other = owner(z, s)
        next_to.append((2 * dz + xl, 2 * lax.rem(plane + PLANES - back, PLANES) + flip(s // 2, other), slot))
    home = step // 2
    mine = flip(core, home)
    sign = 2 * lax.rem(z, 2) - 1
    last = jnp.where(step == STEPS - 1, 1, 0)
    n_frame = lax.rem(step + 1, STEPS)
    n_tmid = 2 * lax.rem(plane + last, PLANES) + n_frame // 2
    cur_of, next_of = [], []
    for s in range(2):
        away = mine if s == 0 else 3 - mine
        zt = 2 * lax.rem(z + sign * away + ROWS, ROWS) + xl
        cur_of.append((zt, 2 * plane + home))
        next_of.append((zt, n_tmid))

    barrier = pltpu.get_barrier_semaphore()

    def greet(t, m):
        other = (t != track) | (m != tm)

        @pl.when(other)
        def _():
            pl.semaphore_signal(barrier, inc=1, device_id=(t, m), device_id_type=MESH)

        return jnp.where(other, 1, 0)

    met = n_track - 1 + n_tm - 1
    for t, m, _ in cur_to + next_to:
        met = met + greet(t, m)
    for t, m in cur_of + next_of:
        met = met + greet(t, m)
    for k in range(1, n_track):
        pl.semaphore_signal(barrier, inc=1, device_id=(lax.rem(track + k, n_track), tm), device_id_type=MESH)
    for k in range(1, n_tm):
        pl.semaphore_signal(barrier, inc=1, device_id=(track, lax.rem(tm + k, n_tm)), device_id_type=MESH)

    acc[...] = jnp.zeros_like(acc)
    ge[...] = jnp.zeros_like(ge)
    en[...] = jnp.zeros_like(en)
    pl.semaphore_wait(barrier, met)

    def send(src, dst, ssem, rsem, t, m, start=True):
        same = (t == track) & (m == tm)
        if start:

            @pl.when(same)
            def _():
                pltpu.make_async_copy(src, dst, rsem).start()

        @pl.when(jnp.logical_not(same))
        def _():
            there = pltpu.make_async_remote_copy(
                src_ref=src, dst_ref=dst, send_sem=ssem, recv_sem=rsem, device_id=(t, m), device_id_type=MESH
            )
            there.start() if start else there.wait_send()

    def arrive(ref, sem):
        pltpu.make_async_copy(ref, ref, sem).wait()

    def stage1(start):
        for l in range(2):
            t, m, slot = cur_to[l]
            tn, mn, slot_n = next_to[l]
            send(pm_ref.at[l], buf.at[0, slot, pl.ds(emb, 8)], s1.at[0, l], r1.at[0, slot], t, m, start)
            send(pm_ref.at[l], buf.at[0, slot_n, pl.ds(emb + 8, 8)], s1.at[1, l], r1.at[1, slot_n], tn, mn, start)
            send(e_ref.at[l], buf.at[0, slot, pl.ds(0, emb)], s1.at[2, l], r1.at[2, slot], t, m, start)

    peers = {
        1: (track, flip(core, 1) + 2 * plane),
        2: (2 * z + 1 - xl, tm),
        4: (2 * (z - sign * 1) + xl, tm),
    }

    def pass_on(n, src, dst, slot, via):
        t, m = peers[via]
        return pltpu.make_async_remote_copy(
            src_ref=buf.at[src, slot], dst_ref=buf.at[dst, slot], send_sem=sg.at[n], recv_sem=rg.at[dst, slot],
            device_id=(t, m), device_id_type=MESH,
        )

    first = [[pass_on(3 * s + k, 0, v, s, v) for k, v in enumerate((2, 4, 1))] for s in range(2)]
    second = [pass_on(6 + s, 2, 3, s, 1) for s in range(2)] + [pass_on(8 + s, 4, 5, s, 1) for s in range(2)]
    across = [pass_on(10, 2, 6, 0, 4), pass_on(11, 4, 6, 1, 2)]
    third = [pass_on(12 + s, 6, 7, s, 1) for s in range(2)]

    stage1(True)
    for s in range(2):
        arrive(buf.at[0, s, pl.ds(emb, 8)], r1.at[0, s])
        arrive(buf.at[0, s, pl.ds(emb + 8, 8)], r1.at[1, s])
        arrive(buf.at[0, s, pl.ds(0, emb)], r1.at[2, s])
        for c in first[s]:
            c.start()
    valid = jnp.where((plane == PLANES - 1) & (step == STEPS - 1), 0.0, 1.0)
    prep_rows(valid, emb, width, buf, mid, ll, ld, tp)

    def landed(u):
        for s in range(2):
            arrive(buf.at[u, s], rg.at[u, s])

    @pl.loop(0, 8)
    def _(i):
        u = i + jnp.where(i == 3, 1, 0) - jnp.where(i == 4, 1, 0)

        @pl.when(i == 1)
        def _():
            landed(1)

        @pl.when(i == 2)
        def _():
            landed(2)
            across[0].start()
            second[0].start()
            second[1].start()
            landed(4)
            across[1].start()
            second[2].start()
            second[3].start()

        @pl.when(i == 4)
        def _():
            landed(6)
            third[0].start()
            third[1].start()
            landed(3)

        @pl.when(i == 5)
        def _():
            landed(5)

        @pl.when(i == 7)
        def _():
            landed(7)

        prep_cols(u, emb, width, buf, pc, mid, rhs, rd)
        unit(u, R, emb, width, pc, rhs, rd, ll, ld, scs, acc, ge, en)

    def round_of(n, group, here, size, send_at):
        return [
            pltpu.make_async_remote_copy(
                src_ref=group.at[here], dst_ref=group.at[here], send_sem=sl.at[n, k - 1], recv_sem=rl.at[n, here],
                device_id=send_at(lax.rem(here + k, size)), device_id_type=MESH,
            )
            for k in range(1, size)
        ]

    def gathered(n, group, here, size):
        for k in range(1, size):
            at = lax.rem(here + k, size)
            arrive(group.at[at], rl.at[n, at])

    l1[track] = en[...]
    round1 = round_of(0, l1, track, n_track, lambda t: (t, tm))
    for c in round1:
        c.start()

    finish(weight, emb, width, acc, ge, tp, gres, pres)

    def stage3(start):
        for s in range(2):
            t, m = cur_of[s]
            tn, mn = next_of[s]
            l = lax.rem(step, 2)
            ln = lax.rem(n_frame, 2)
            send(pres.at[s, 0], prec.at[l, 0], sr.at[0, s], rr.at[0, l], t, m, start)
            send(pres.at[s, 1], prec.at[ln, 1], sr.at[1, s], rr.at[1, ln], tn, mn, start)
            send(gres.at[s], gemb.at[l], sr.at[2, s], rr.at[2, l], t, m, start)

    stage3(True)
    gathered(0, l1, track, n_track)
    l2[tm] = jnp.sum(l1[...], axis=0)
    round2 = round_of(1, l2, tm, n_tm, lambda m: (track, m))
    for c in round2:
        c.start()
    for l in range(2):
        arrive(prec.at[l, 0], rr.at[0, l])
        arrive(prec.at[l, 1], rr.at[1, l])
        gpos[l] = prec[l, 0] + prec[l, 1]
        arrive(gemb.at[l], rr.at[2, l])
    gathered(1, l2, tm, n_tm)
    pairs = tracks * (tracks - 1) / 2.0 * (frames - 1)
    total = jnp.sum(jnp.sum(jnp.sum(l2[...], axis=0), axis=0, keepdims=True), axis=1, keepdims=True)
    lout[...] = jnp.broadcast_to(total * (0.25 / pairs), lout.shape)

    stage1(False)
    for c in first[0] + first[1] + second + across + third + round1 + round2:
        c.wait_send()
    stage3(False)


def on_device(positions, embeddings, visible):
    frames_local, emb, width = embeddings.shape
    tracks = width * lax.axis_size("track")
    frames = frames_local * lax.axis_size("tm")
    seen = visible.astype(f32)
    pm = jnp.concatenate(
        [jnp.swapaxes(positions, 0, 1), seen[:, None], jnp.zeros((frames_local, 4, width), f32)], 1
    )
    R = width // 2
    C = 2 * width
    K = 3 * emb + LANE
    dma, vmem = pltpu.SemaphoreType.DMA, pltpu.VMEM
    scratch = [
        vmem((8, 2, emb + 16, width), f32),
        vmem((8, 2, 16, width), f32),
        vmem((16, LANE), f32),
        vmem((8, K, C), bf16),
        vmem((8, 2, 32, C), bf16),
        vmem((C, K), bf16),
        vmem((2, C, 32), bf16),
        vmem((2, C, LANE), f32),
        vmem((8, C, LANE), f32),
        vmem((C, emb), f32),
        vmem((8, LANE), f32),
        vmem((2, emb, width), f32),
        vmem((2, 2, 8, width), f32),
        vmem((2, 2, 8, width), f32),
        vmem((16, 8, LANE), f32),
        vmem((16, 8, LANE), f32),
    ]
    for _ in range(NBUF):
        scratch += [vmem((R, C), f32)] * 3 + [vmem((2 * R, C), bf16)]
    scratch += [dma((3, 2)), dma((3, 2)), dma((8, 2)), dma((14,)), dma((3, 2)), dma((3, 2)), dma((2, 16)), dma((2, 15))]
    whole = pl.BlockSpec(memory_space=pltpu.VMEM)
    grad_emb, grad_pos, loss = pl.pallas_call(
        functools.partial(kernel, R, emb, width, tracks, frames),
        out_shape=[
            jax.ShapeDtypeStruct((2, emb, width), f32),
            jax.ShapeDtypeStruct((2, 8, width), f32),
            jax.ShapeDtypeStruct((8, LANE), f32),
        ],
        in_specs=[whole, whole],
        out_specs=[whole] * 3,
        scratch_shapes=scratch,
        compiler_params=pltpu.CompilerParams(
            collective_id=0, has_side_effects=True, vmem_limit_bytes=60 * 2**20
        ),
    )(embeddings, pm)
    return (jnp.swapaxes(grad_pos[:, :3], 0, 1), grad_emb, loss[0, 0])


def solution(mesh):
    in_specs = (P(None, "tm", "track"), P("tm", None, "track"), P("tm", "track"))
    out_specs = (P(None, "tm", "track"), P("tm", None, "track"), P())
    return jax.shard_map(
        on_device, mesh=mesh, in_specs=in_specs, out_specs=out_specs, check_vma=False
    )
```

time: 586 us -> 78.9 us (0.13)
  the two profiles are of different devices: /device:TPU:6 before, /device:TPU:32 now
where the time goes in v1:
time: 78.9 us; the launch traced here: 78.6 us
  Pallas kernels  72.3 us (92%)
  local copies, waits for them, and re-layouts  4.99 us (6%)
    pallas_call x1, Pallas kernels, on_device(): pl.pallas_call(functools.partial(kernel, R, emb, width, tracks, frames),...  72.3 us
    unnamed x7, local copies, waits for them, and re-layouts  2.98 us

profile of v1, /device:TPU:32, one launch (start us, length us, event | category | flops | bytes accessed | tf_op | source)
XLA Modules:
  0.0 78.6 jit_solution(5580552604354668055)
XLA Ops:
  0.6 0.0 copy-start.1
  0.6 0.0 copy-start
  0.7 0.1 pad.2.clone
  0.7 0.6 copy-done.1
  1.3 0.0 copy-done
  1.4 0.7 maximum_maximum_fusion.pm_ref
  2.0 72.3 %shard_map.58 = (f32[2,128,384]{2,1,0:T(8,128)}, f32[2,8,384]{2,1,0:T(8,128)}, f32[8,128]{1,0:T(8,128)}) custom-call(f32[2,128,384]{2,1,0:T(8,128)} %e_ref.1, f32[2,8,384]{2,1,0:T(8,128)} %maximum_maximum_fusion.pm_ref), custom_call_target="tpu_custom_call" | custom-call | tf_op jit(solution)/shard_map/pallas_call | solution.py:429
  74.3 1.2 %slice.7 = f32[1,1]{1,0:T(1,128)} slice(f32[8,128]{1,0:T(8,128)} %get-tuple-element.8), slice={[0:1], [0:1]} | slice | bytes 8 | tf_op jit(solution)/shard_map/slice | solution.py:443
  75.5 0.7 slice_bitcast_fusion
  76.2 0.6 copy.7
  76.8 1.8 %copy.11 = f32[2,128,384]{2,1,0:T(8,128)} copy(f32[2,128,384]{2,1,0:T(8,128)} %get-tuple-element.16) | data formatting | bytes 786432
  (4 shorter events, 0.0 us)
Async XLA Ops:
  0.6 0.7 copy-start.1
  0.6 0.7 copy-start

commit v2 on v1

--- a/solution.py
+++ b/solution.py
@@ -13,6 +13,7 @@
 rigidity = 4.0
 HIDE = 2.0**20
 LANE = 128
+ENERGY = True
 NBUF = 2
 
 ROWS = 8
@@ -44,17 +45,19 @@
     return h, m, (v - h - m).astype(bf16).astype(f32)
 
 
-def prep_cols(u, emb, width, buf, pc, mid, rhs, rd):
-    for s in range(2):
-        cs = slice(s * width, (s + 1) * width)
+def prep_cols(chip, s, emb, width, buf, pc, mid, rhs, rd):
+    g = 2 * chip + s
+    for half in range(2):
+        u = 2 * chip + half
+        cs = slice(half * width, (half + 1) * width)
         hi, lo = split2(buf[u, s, 0:emb, :])
-        rhs[u, 0:emb, cs] = hi
-        rhs[u, emb : 2 * emb, cs] = lo
-        rhs[u, 2 * emb : 3 * emb, cs] = hi
+        rhs[g, 0:emb, cs] = hi
+        rhs[g, emb : 2 * emb, cs] = lo
+        rhs[g, 2 * emb : 3 * emb, cs] = hi
         q = buf[u, s, emb + 3 : emb + 4, :] * buf[u, s, emb + 11 : emb + 12, :]
         rows = lax.broadcasted_iota(jnp.int32, (LANE, width), 0)
         m = jnp.where(rows == 0, 1.0, 0.0) + jnp.where(rows == 1, (q - 1.0) * HIDE, 0.0)
-        rhs[u, 3 * emb :, cs] = m.astype(bf16)
+        rhs[g, 3 * emb :, cs] = m.astype(bf16)
         for f in range(2):
             p = [
                 buf[u, s, emb + 8 * f + c : emb + 8 * f + c + 1, :] - mid[8 * f + c : 8 * f + c + 1, 0:1]
@@ -62,19 +65,20 @@
             ]
             out = []
             for c in range(3):
-                pc[u, s, 8 * f + c : 8 * f + c + 1, :] = p[c]
+                pc[g, half, 8 * f + c : 8 * f + c + 1, :] = p[c]
                 h, mm, l = pieces(p[c])
                 out += [h, mm, h, mm, l, h]
             n = p[0] * p[0] + p[1] * p[1] + p[2] * p[2]
             one = jnp.ones_like(n)
             out += [one, one, one] + list(pieces(n)) + [jnp.zeros((8, width), f32)]
-            rd[u, f, :, cs] = jnp.concatenate(out, 0).astype(bf16)
-
-
-def prep_rows(valid, emb, width, buf, mid, ll, ld, tp):
-    mean = (jnp.sum(buf[0, 0, emb:, :], 1, keepdims=True) + jnp.sum(buf[0, 1, emb:, :], 1, keepdims=True)) / (2.0 * width)
-    mid[...] = jnp.broadcast_to(mean, mid.shape)
-    for s in range(2):
+            rd[g, f, :, cs] = jnp.concatenate(out, 0).astype(bf16)
+
+
+def prep_rows(sides, valid, emb, width, buf, mid, ll, ld, tp):
+    if 0 in sides:
+        mean = jnp.sum(buf[0, 0, emb:, :], 1, keepdims=True) / width
+        mid[...] = jnp.broadcast_to(mean, mid.shape)
+    for s in sides:
         rs = slice(s * width, (s + 1) * width)
         hi, lo = split2(jnp.transpose(buf[0, s, 0:emb, :]) * (0.5 / math.sqrt(emb)))
         ll[rs, 0:emb] = hi
@@ -99,21 +103,24 @@
             tp[f, rs, :] = jnp.transpose(jnp.concatenate(p + [jnp.zeros((LANE - 3, width), f32)], 0))
 
 
-def dot_piece(k, n, u, r0, R, rhs, rd, ll, ld, sc):
-    ns = slice(n, n + 256)
+def dot_piece(k, n0, n1, u, r0, R, rhs, rd, ll, ld, sc):
+    ns = slice(n0, n1)
+    rows = slice(r0, r0 + R)
     if k == 0:
-        sc[0][:, ns] = jnp.dot(ll[r0 : r0 + R, :], rhs[u, :, ns], preferred_element_type=f32)
+        sc[0][:, ns] = jnp.dot(ll[rows, :], rhs[u, :, ns], preferred_element_type=f32)
     else:
-        sc[k][:, ns] = jnp.dot(ld[k - 1, r0 : r0 + R, :], rd[u, k - 1, :, ns], preferred_element_type=f32)
-
-
-def strip(s, u, r0, R, width, pc, acc, en, sc):
+        sc[k][:, ns] = jnp.dot(ld[k - 1, rows, :], rd[u, k - 1, :, ns], preferred_element_type=f32)
+
+
+def strip(s, u, r0, cols, width, pc, acc, en, energy, sc):
     xs, d0s, d1s, gs = sc
-    A = [acc[k, r0 + s : r0 + s + 16, :] for k in range(8)]
-    es = en[...]
-    span = 256
-    for c0 in range(0, 2 * width, span):
-        cs = slice(c0, c0 + span)
+    R = xs.shape[0]
+    at = slice(r0 + s, r0 + s + 16)
+    A = [acc[k, at, :] for k in range(8)]
+    es = en[...] if energy else None
+    for c0 in range(cols[0], cols[1], 256):
+        c1 = min(c0 + 256, cols[1])
+        cs = slice(c0, c1)
         x, a0, a1 = xs[s : s + 16, cs], d0s[s : s + 16, cs], d1s[s : s + 16, cs]
         q0, q1 = lax.rsqrt(a0), lax.rsqrt(a1)
         ch = a1 * q1 - a0 * q0
@@ -123,9 +130,9 @@
         hi = g.astype(bf16)
         gs[s : s + 16, cs] = hi
         gs[R + s : R + s + 16, cs] = (g - hi.astype(f32)).astype(bf16)
-        e = h * ch
+        e = h * ch if energy else None
         w = (h * q0, h * q1)
-        for k in range(0, span, LANE):
+        for k in range(0, c1 - c0, LANE):
             j = c0 + k
             side, js = j // width, slice(j % width, j % width + LANE)
             for f in range(2):
@@ -133,41 +140,46 @@
                 A[4 * f] = A[4 * f] + wk
                 for c in range(3):
                     A[4 * f + 1 + c] = A[4 * f + 1 + c] + wk * pc[u, side, 8 * f + c : 8 * f + c + 1, js]
-            es = es + (e[0:8, k : k + LANE] + e[8:16, k : k + LANE])
+            if energy:
+                es = es + (e[0:8, k : k + LANE] + e[8:16, k : k + LANE])
     for k in range(8):
-        acc[k, r0 + s : r0 + s + 16, :] = A[k]
-    en[...] = es
-
-
-def grad_dot(u, r0, R, emb, rhs, ge, sc):
+        acc[k, at, :] = A[k]
+    if energy:
+        en[...] = es
+
+
+def grad_dot(u, r0, cols, emb, rhs, ge, sc):
+    R = sc[0].shape[0]
+    cs = slice(*cols)
     o = lax.dot_general(
-        sc[3][...], rhs[u, 0 : 2 * emb, :], (((1,), (1,)), ((), ())), preferred_element_type=f32
+        sc[3][:, cs], rhs[u, 0 : 2 * emb, cs], (((1,), (1,)), ((), ())), preferred_element_type=f32
     )
-    ge[r0 : r0 + R, :] = ge[r0 : r0 + R, :] + ((o[:R, :emb] + o[:R, emb:]) + o[R:, :emb])
-
-
-def unit(u, R, emb, width, pc, rhs, rd, ll, ld, scs, acc, ge, en):
-    todo = [(k, n) for n in range(0, 2 * width, 256) for k in range(3)]
-    chunks = list(range(0, 2 * width, R))
+    rows = slice(r0, r0 + R)
+    ge[rows, :] = ge[rows, :] + ((o[:R, :emb] + o[:R, emb:]) + o[R:, :emb])
+
+
+def tiles(jobs, energy, emb, width, pc, rhs, rd, ll, ld, scs, acc, ge, en):
+    R = scs[0][0].shape[0]
+    cols = (0, 2 * width)
+    parts = [(k, n, n + 256) for n in range(0, 2 * width, 256) for k in range(3)]
     strips = list(range(0, R, 16))
-    per = -(-len(todo) // len(strips))
-    for k, n in todo:
-        dot_piece(k, n, u, chunks[0], R, rhs, rd, ll, ld, scs[0])
-    for i, r0 in enumerate(chunks):
-        later = list(todo) if i + 1 < len(chunks) else []
+    for part in parts:
+        dot_piece(*part, jobs[0][1], jobs[0][0], R, rhs, rd, ll, ld, scs[0])
+    for i, (r0, u) in enumerate(jobs):
+        later = list(parts) if i + 1 < len(jobs) else []
+        per = -(-len(later) // len(strips))
         for j, s in enumerate(strips):
-            strip(s, u, r0, R, width, pc, acc, en, scs[i % NBUF])
+            strip(s, u, r0, cols, width, pc, acc, en, energy, scs[i % NBUF])
             if j == 0 and i > 0:
-                grad_dot(u, chunks[i - 1], R, emb, rhs, ge, scs[(i - 1) % NBUF])
+                grad_dot(jobs[i - 1][1], jobs[i - 1][0], cols, emb, rhs, ge, scs[(i - 1) % NBUF])
             for _ in range(per):
                 if later:
-                    k, n = later.pop(0)
-                    dot_piece(k, n, u, chunks[i + 1], R, rhs, rd, ll, ld, scs[(i + 1) % NBUF])
-    grad_dot(u, chunks[-1], R, emb, rhs, ge, scs[(len(chunks) - 1) % NBUF])
-
-
-def finish(weight, emb, width, acc, ge, tp, gres, pres):
-    for s in range(2):
+                    dot_piece(*later.pop(0), jobs[i + 1][1], jobs[i + 1][0], R, rhs, rd, ll, ld, scs[(i + 1) % NBUF])
+    grad_dot(jobs[-1][1], jobs[-1][0], cols, emb, rhs, ge, scs[(len(jobs) - 1) % NBUF])
+
+
+def finish(sides, weight, emb, width, acc, ge, tp, gres, pres):
+    for s in sides:
         rs = slice(s * width, (s + 1) * width)
         gres[s] = jnp.transpose(ge[rs, :]) * (weight / (4.0 * math.sqrt(emb)))
         cols = lax.broadcasted_iota(jnp.int32, (width, LANE), 1)
@@ -183,8 +195,8 @@
 
 def kernel(
     R, emb, width, tracks, frames,
-    e_ref, pm_ref, gemb, gpos, lout,
-    buf, pc, mid, rhs, rd, ll, ld, tp, acc, ge, en, gres, pres, prec, l1, l2,
+    pos, emb_in, vis, gpos, gemb, lout,
+    pos_v, vis_v, e_ref, pm_ref, sin, buf, pc, mid, rhs, rd, ll, ld, tp, acc, ge, en, ent, gres, pres, prec, l1, l2,
     *rest,
 ):
     scs = [rest[4 * i : 4 * i + 4] for i in range(NBUF)]
@@ -239,9 +251,22 @@
     for k in range(1, n_tm):
         pl.semaphore_signal(barrier, inc=1, device_id=(track, lax.rem(tm + k, n_tm)), device_id_type=MESH)
 
+    bring = [
+        pltpu.make_async_copy(pos, pos_v, sin.at[0]),
+        pltpu.make_async_copy(vis, vis_v, sin.at[1]),
+        pltpu.make_async_copy(emb_in, e_ref, sin.at[2]),
+    ]
+    for c in bring:
+        c.start()
     acc[...] = jnp.zeros_like(acc)
     ge[...] = jnp.zeros_like(ge)
     en[...] = jnp.zeros_like(en)
+    ent[...] = jnp.zeros_like(ent)
+    for c in bring:
+        c.wait()
+    for l in range(2):
+        rows = [pos_v[c, l : l + 1, :] for c in range(3)] + [vis_v[l : l + 1, :].astype(f32)]
+        pm_ref[l] = jnp.concatenate(rows + [jnp.zeros((4, width), f32)], 0)
     pl.semaphore_wait(barrier, met)
 
     def send(src, dst, ssem, rsem, t, m, start=True):
@@ -268,7 +293,18 @@
             tn, mn, slot_n = next_to[l]
             send(pm_ref.at[l], buf.at[0, slot, pl.ds(emb, 8)], s1.at[0, l], r1.at[0, slot], t, m, start)
             send(pm_ref.at[l], buf.at[0, slot_n, pl.ds(emb + 8, 8)], s1.at[1, l], r1.at[1, slot_n], tn, mn, start)
-            send(e_ref.at[l], buf.at[0, slot, pl.ds(0, emb)], s1.at[2, l], r1.at[2, slot], t, m, start)
+
+    def stage1_emb(slots, start):
+        for l in range(2):
+            t, m, slot = cur_to[l]
+
+            def go():
+                send(e_ref.at[l], buf.at[0, slot, pl.ds(0, emb)], s1.at[2, l], r1.at[2, slot], t, m, start)
+
+            if slots is None:
+                go()
+            else:
+                pl.when(slot == slots)(go)
 
     peers = {
         1: (track, flip(core, 1) + 2 * plane),
@@ -288,56 +324,31 @@
     across = [pass_on(10, 2, 6, 0, 4), pass_on(11, 4, 6, 1, 2)]
     third = [pass_on(12 + s, 6, 7, s, 1) for s in range(2)]
 
+    stage1_emb(0, True)
     stage1(True)
-    for s in range(2):
+    valid = jnp.where((plane == PLANES - 1) & (step == STEPS - 1), 0.0, 1.0)
+
+    def own(s):
         arrive(buf.at[0, s, pl.ds(emb, 8)], r1.at[0, s])
         arrive(buf.at[0, s, pl.ds(emb + 8, 8)], r1.at[1, s])
         arrive(buf.at[0, s, pl.ds(0, emb)], r1.at[2, s])
         for c in first[s]:
             c.start()
-    valid = jnp.where((plane == PLANES - 1) & (step == STEPS - 1), 0.0, 1.0)
-    prep_rows(valid, emb, width, buf, mid, ll, ld, tp)
-
-    def landed(u):
-        for s in range(2):
-            arrive(buf.at[u, s], rg.at[u, s])
-
-    @pl.loop(0, 8)
-    def _(i):
-        u = i + jnp.where(i == 3, 1, 0) - jnp.where(i == 4, 1, 0)
-
-        @pl.when(i == 1)
-        def _():
-            landed(1)
-
-        @pl.when(i == 2)
-        def _():
-            landed(2)
-            across[0].start()
-            second[0].start()
-            second[1].start()
-            landed(4)
-            across[1].start()
-            second[2].start()
-            second[3].start()
-
-        @pl.when(i == 4)
-        def _():
-            landed(6)
-            third[0].start()
-            third[1].start()
-            landed(3)
-
-        @pl.when(i == 5)
-        def _():
-            landed(5)
-
-        @pl.when(i == 7)
-        def _():
-            landed(7)
-
-        prep_cols(u, emb, width, buf, pc, mid, rhs, rd)
-        unit(u, R, emb, width, pc, rhs, rd, ll, ld, scs, acc, ge, en)
+        prep_rows((s,), valid, emb, width, buf, mid, ll, ld, tp)
+
+    def landed(u, s):
+        arrive(buf.at[u, s], rg.at[u, s])
+
+    own(0)
+
+    def stage3(s, start):
+        t, m = cur_of[s]
+        tn, mn = next_of[s]
+        l = lax.rem(step, 2)
+        ln = lax.rem(n_frame, 2)
+        send(gres.at[s], gemb.at[l], sr.at[2, s], rr.at[2, l], t, m, start)
+        send(pres.at[s, 0], prec.at[l, 0], sr.at[0, s], rr.at[0, l], t, m, start)
+        send(pres.at[s, 1], prec.at[ln, 1], sr.at[1, s], rr.at[1, ln], tn, mn, start)
 
     def round_of(n, group, here, size, send_at):
         return [
@@ -353,58 +364,127 @@
             at = lax.rem(here + k, size)
             arrive(group.at[at], rl.at[n, at])
 
-    l1[track] = en[...]
+    cols = (emb, width, buf, pc, mid, rhs, rd)
+    work = (emb, width, pc, rhs, rd, ll, ld, scs, acc, ge, en)
+
+    @pl.loop(0, 4)
+    def _(chip):
+        @pl.when(chip == 0)
+        def _():
+            landed(1, 0)
+            stage1_emb(1, True)
+
+        @pl.when(chip == 1)
+        def _():
+            landed(2, 0)
+            across[0].start()
+            second[0].start()
+            landed(4, 0)
+            second[2].start()
+            landed(3, 0)
+
+        @pl.when(chip == 2)
+        def _():
+            landed(5, 0)
+
+        @pl.when(chip == 3)
+        def _():
+            landed(6, 0)
+            third[0].start()
+            own(1)
+            landed(7, 0)
+
+        prep_cols(chip, 0, *cols)
+        tiles([(0, 2 * chip)], True, *work)
+
+    ent[...] = en[...]
+    en[...] = jnp.zeros_like(en)
+
+    @pl.loop(0, 4)
+    def _(i):
+        @pl.when(i == 1)
+        def _():
+            landed(2, 1)
+            second[1].start()
+            landed(4, 1)
+            across[1].start()
+            second[3].start()
+
+        @pl.when(i == 2)
+        def _():
+            landed(1, 1)
+            landed(3, 1)
+            prep_cols(0, 1, *cols)
+            prep_cols(1, 1, *cols)
+            ent[...] = ent[...] + 2.0 * en[...]
+            en[...] = jnp.zeros_like(en)
+
+        @pl.when(i == 3)
+        def _():
+            landed(6, 1)
+            third[1].start()
+            landed(5, 1)
+            prep_cols(2, 1, *cols)
+            landed(7, 1)
+            prep_cols(3, 1, *cols)
+
+        g = 4 * lax.rem(i, 2) + i // 2
+        tiles([(width, g), (width, g + 2)], True, *work)
+
+    l1[track] = ent[...] + en[...]
+    finish((1,), weight, emb, width, acc, ge, tp, gres, pres)
     round1 = round_of(0, l1, track, n_track, lambda t: (t, tm))
+    round2 = round_of(1, l2, tm, n_tm, lambda m: (track, m))
     for c in round1:
         c.start()
-
-    finish(weight, emb, width, acc, ge, tp, gres, pres)
-
-    def stage3(start):
-        for s in range(2):
-            t, m = cur_of[s]
-            tn, mn = next_of[s]
-            l = lax.rem(step, 2)
-            ln = lax.rem(n_frame, 2)
-            send(pres.at[s, 0], prec.at[l, 0], sr.at[0, s], rr.at[0, l], t, m, start)
-            send(pres.at[s, 1], prec.at[ln, 1], sr.at[1, s], rr.at[1, ln], tn, mn, start)
-            send(gres.at[s], gemb.at[l], sr.at[2, s], rr.at[2, l], t, m, start)
-
-    stage3(True)
-    gathered(0, l1, track, n_track)
-    l2[tm] = jnp.sum(l1[...], axis=0)
-    round2 = round_of(1, l2, tm, n_tm, lambda m: (track, m))
-    for c in round2:
-        c.start()
+    stage3(1, True)
+
+    @pl.loop(0, 2)
+    def _(i):
+        @pl.when(i == 1)
+        def _():
+            gathered(0, l1, track, n_track)
+            l2[tm] = jnp.sum(l1[...], axis=0)
+            for c in round2:
+                c.start()
+
+        tiles([(0, 4 * i + 1), (0, 4 * i + 3)], ENERGY, *work)
+
+    finish((0,), weight, emb, width, acc, ge, tp, gres, pres)
+    stage3(0, True)
     for l in range(2):
         arrive(prec.at[l, 0], rr.at[0, l])
         arrive(prec.at[l, 1], rr.at[1, l])
-        gpos[l] = prec[l, 0] + prec[l, 1]
+        for c in range(3):
+            gpos[c, l : l + 1, :] = prec[l, 0, c : c + 1, :] + prec[l, 1, c : c + 1, :]
         arrive(gemb.at[l], rr.at[2, l])
     gathered(1, l2, tm, n_tm)
     pairs = tracks * (tracks - 1) / 2.0 * (frames - 1)
     total = jnp.sum(jnp.sum(jnp.sum(l2[...], axis=0), axis=0, keepdims=True), axis=1, keepdims=True)
-    lout[...] = jnp.broadcast_to(total * (0.25 / pairs), lout.shape)
+    lout[...] = total * (0.25 / pairs)
 
     stage1(False)
+    stage1_emb(None, False)
     for c in first[0] + first[1] + second + across + third + round1 + round2:
         c.wait_send()
-    stage3(False)
+    for s in range(2):
+        stage3(s, False)
 
 
 def on_device(positions, embeddings, visible):
     frames_local, emb, width = embeddings.shape
     tracks = width * lax.axis_size("track")
     frames = frames_local * lax.axis_size("tm")
-    seen = visible.astype(f32)
-    pm = jnp.concatenate(
-        [jnp.swapaxes(positions, 0, 1), seen[:, None], jnp.zeros((frames_local, 4, width), f32)], 1
-    )
-    R = width // 2
+    R = width
     C = 2 * width
     K = 3 * emb + LANE
     dma, vmem = pltpu.SemaphoreType.DMA, pltpu.VMEM
     scratch = [
+        vmem((3, 2, width), f32),
+        vmem((2, width), jnp.int32),
+        vmem((2, emb, width), f32),
+        vmem((2, 8, width), f32),
+        dma((3,)),
         vmem((8, 2, emb + 16, width), f32),
         vmem((8, 2, 16, width), f32),
         vmem((16, LANE), f32),
@@ -416,6 +496,7 @@
         vmem((8, C, LANE), f32),
         vmem((C, emb), f32),
         vmem((8, LANE), f32),
+        vmem((8, LANE), f32),
         vmem((2, emb, width), f32),
         vmem((2, 2, 8, width), f32),
         vmem((2, 2, 8, width), f32),
@@ -425,22 +506,22 @@
     for _ in range(NBUF):
         scratch += [vmem((R, C), f32)] * 3 + [vmem((2 * R, C), bf16)]
     scratch += [dma((3, 2)), dma((3, 2)), dma((8, 2)), dma((14,)), dma((3, 2)), dma((3, 2)), dma((2, 16)), dma((2, 15))]
-    whole = pl.BlockSpec(memory_space=pltpu.VMEM)
-    grad_emb, grad_pos, loss = pl.pallas_call(
+    whole, there = pl.BlockSpec(memory_space=pltpu.VMEM), pl.BlockSpec(memory_space=pl.ANY)
+    grad_pos, grad_emb, loss = pl.pallas_call(
         functools.partial(kernel, R, emb, width, tracks, frames),
         out_shape=[
+            jax.ShapeDtypeStruct((3, 2, width), f32),
             jax.ShapeDtypeStruct((2, emb, width), f32),
-            jax.ShapeDtypeStruct((2, 8, width), f32),
-            jax.ShapeDtypeStruct((8, LANE), f32),
+            jax.ShapeDtypeStruct((1, 1), f32),
         ],
-        in_specs=[whole, whole],
+        in_specs=[there] * 3,
         out_specs=[whole] * 3,
         scratch_shapes=scratch,
         compiler_params=pltpu.CompilerParams(
             collective_id=0, has_side_effects=True, vmem_limit_bytes=60 * 2**20
         ),
-    )(embeddings, pm)
-    return (jnp.swapaxes(grad_pos[:, :3], 0, 1), grad_emb, loss[0, 0])
+    )(positions, embeddings, visible)
+    return (grad_pos, grad_emb, loss.reshape(()))
 
 
 def solution(mesh):

time: 78.9 us -> 76.7 us (0.972)
  the two profiles are of different devices: /device:TPU:32 before, /device:TPU:6 now
where the time goes in v2:
time: 76.7 us; the launch traced here: 76.5 us
  Pallas kernels  71 us (93%)
  local copies, waits for them, and re-layouts  3.07 us (4%)
  between operations  2.46 us (3%)
    pallas_call x1, Pallas kernels, on_device(): pl.pallas_call(functools.partial(kernel, R, emb, width, tracks, frames),...  71 us
    unnamed x2, local copies, waits for them, and re-layouts  3.07 us

profile of v2, /device:TPU:6, one launch (start us, length us, event | category | flops | bytes accessed | tf_op | source)
XLA Modules:
  0.0 76.5 jit_solution(17806457809339720430)
XLA Ops:
  0.6 71.0 %shard_map.58 = (f32[3,2,384]{2,1,0:T(2,128)}, f32[2,128,384]{2,1,0:T(8,128)}, f32[1,1]{1,0:T(1,128)}) custom-call(f32[3,2,384]{2,1,0:T(2,128)} %pos.1, f32[2,128,384]{2,1,0:T(8,128)} %emb_in.1, s32[2,384]{1,0:T(2,128)} %vis.1), custom_call_target="tpu_custom_call" | custom-call | tf_op jit(solution)/shard_map/pallas_call | solution.py:510
  71.6 1.3 %copy.9 = f32[3,2,384]{2,1,0:T(2,128)} copy(f32[3,2,384]{2,1,0:T(2,128)} %get-tuple-element.12) | data formatting | bytes 18432
  72.9 1.8 %copy.10 = f32[2,128,384]{2,1,0:T(8,128)} copy(f32[2,128,384]{2,1,0:T(8,128)} %get-tuple-element.13) | data formatting | bytes 786432

commit v3 on v2

--- a/solution.py
+++ b/solution.py
@@ -510,9 +510,9 @@
     grad_pos, grad_emb, loss = pl.pallas_call(
         functools.partial(kernel, R, emb, width, tracks, frames),
         out_shape=[
-            jax.ShapeDtypeStruct((3, 2, width), f32),
-            jax.ShapeDtypeStruct((2, emb, width), f32),
-            jax.ShapeDtypeStruct((1, 1), f32),
+            vmem((3, 2, width), f32),
+            vmem((2, emb, width), f32),
+            vmem((1, 1), f32),
         ],
         in_specs=[there] * 3,
         out_specs=[whole] * 3,

time: 76.7 us -> 73.3 us (0.956)
  local copies, waits for them, and re-layouts: 3.07 us -> 1.35 us
  Pallas kernels: 71 us -> 70.1 us
    unnamed x2, local copies, waits for them, and re-layouts: 3.07 us -> 1.35 us
    pallas_call x1, Pallas kernels: 71 us -> 70.1 us  [on_device(): pl.pallas_call(functools.partial(kernel, R, emb, width, tracks, frames),...]
where the time goes in v3:
time: 73.3 us; the launch traced here: 73.2 us
  Pallas kernels  70.1 us (96%)
  between operations  1.8 us (2%)
  local copies, waits for them, and re-layouts  1.35 us (2%)
    pallas_call x1, Pallas kernels, on_device(): pl.pallas_call(functools.partial(kernel, R, emb, width, tracks, frames),...  70.1 us

profile of v3, /device:TPU:6, one launch (start us, length us, event | category | flops | bytes accessed | tf_op | source)
XLA Modules:
  0.0 73.2 jit_solution(17123531294776232447)
XLA Ops:
  0.6 70.1 %shard_map.58 = (f32[3,2,384]{2,1,0:T(2,128)S(1)}, f32[2,128,384]{2,1,0:T(8,128)S(1)}, f32[1,1]{1,0:T(1,128)S(1)}) custom-call(f32[3,2,384]{2,1,0:T(2,128)} %pos.1, f32[2,128,384]{2,1,0:T(8,128)} %emb_in.1, s32[2,384]{1,0:T(2,128)} %vis.1), custom_call_target="tpu_custom_call" | custom-call | tf_op jit(solution)/shard_map/pallas_call | solution.py:510
  70.7 0.6 copy.9
  71.3 0.7 %copy.10 = f32[2,128,384]{2,1,0:T(8,128)} copy(f32[2,128,384]{2,1,0:T(8,128)S(1)} %get-tuple-element.10) | data formatting | bytes 786432

commit v4 on v3

--- a/solution.py
+++ b/solution.py
@@ -324,8 +324,8 @@
     across = [pass_on(10, 2, 6, 0, 4), pass_on(11, 4, 6, 1, 2)]
     third = [pass_on(12 + s, 6, 7, s, 1) for s in range(2)]
 
+    stage1(True)
     stage1_emb(0, True)
-    stage1(True)
     valid = jnp.where((plane == PLANES - 1) & (step == STEPS - 1), 0.0, 1.0)
 
     def own(s):
@@ -367,7 +367,7 @@
     cols = (emb, width, buf, pc, mid, rhs, rd)
     work = (emb, width, pc, rhs, rd, ll, ld, scs, acc, ge, en)
 
-    @pl.loop(0, 4)
+    @pl.loop(0, 3)
     def _(chip):
         @pl.when(chip == 0)
         def _():
@@ -387,23 +387,26 @@
         def _():
             landed(5, 0)
 
-        @pl.when(chip == 3)
-        def _():
-            landed(6, 0)
-            third[0].start()
-            own(1)
-            landed(7, 0)
-
         prep_cols(chip, 0, *cols)
         tiles([(0, 2 * chip)], True, *work)
 
     ent[...] = en[...]
     en[...] = jnp.zeros_like(en)
+    own(1)
+    landed(6, 0)
+    third[0].start()
 
     @pl.loop(0, 4)
     def _(i):
         @pl.when(i == 1)
         def _():
+            landed(7, 0)
+            prep_cols(3, 0, *cols)
+            ent[...] = ent[...] + 2.0 * en[...]
+            en[...] = jnp.zeros_like(en)
+            tiles([(0, 6)], True, *work)
+            ent[...] = ent[...] + en[...]
+            en[...] = jnp.zeros_like(en)
             landed(2, 1)
             second[1].start()
             landed(4, 1)

time: 73.3 us -> 72.2 us (0.985)
  Pallas kernels: 70.1 us -> 68.4 us
    pallas_call x1, Pallas kernels: 70.1 us -> 68.4 us  [on_device(): pl.pallas_call(functools.partial(kernel, R, emb, width, tracks, frames),...]
where the time goes in v4:
time: 72.2 us; the launch traced here: 71.5 us
  Pallas kernels  68.4 us (95%)
  between operations  1.8 us (2%)
  local copies, waits for them, and re-layouts  1.35 us (2%)
    pallas_call x1, Pallas kernels, on_device(): pl.pallas_call(functools.partial(kernel, R, emb, width, tracks, frames),...  68.4 us

profile of v4, /device:TPU:6, one launch (start us, length us, event | category | flops | bytes accessed | tf_op | source)
XLA Modules:
  0.0 71.5 jit_solution(744044217422134123)
XLA Ops:
  0.6 68.4 %shard_map.58 = (f32[3,2,384]{2,1,0:T(2,128)S(1)}, f32[2,128,384]{2,1,0:T(8,128)S(1)}, f32[1,1]{1,0:T(1,128)S(1)}) custom-call(f32[3,2,384]{2,1,0:T(2,128)} %pos.1, f32[2,128,384]{2,1,0:T(8,128)} %emb_in.1, s32[2,384]{1,0:T(2,128)} %vis.1), custom_call_target="tpu_custom_call" | custom-call | tf_op jit(solution)/shard_map/pallas_call | solution.py:513
  69.1 0.6 copy.9
  69.7 0.7 %copy.10 = f32[2,128,384]{2,1,0:T(8,128)} copy(f32[2,128,384]{2,1,0:T(8,128)S(1)} %get-tuple-element.10) | data formatting | bytes 786432

commit v5 on v4

--- a/solution.py
+++ b/solution.py
@@ -419,13 +419,13 @@
             landed(3, 1)
             prep_cols(0, 1, *cols)
             prep_cols(1, 1, *cols)
+            landed(6, 1)
+            third[1].start()
             ent[...] = ent[...] + 2.0 * en[...]
             en[...] = jnp.zeros_like(en)
 
         @pl.when(i == 3)
         def _():
-            landed(6, 1)
-            third[1].start()
             landed(5, 1)
             prep_cols(2, 1, *cols)
             landed(7, 1)

time: 72.2 us -> 72.6 us (level)
  no operation moved by 1% of the time
where the time goes in v5:
time: 72.6 us; the launch traced here: 71.8 us
  Pallas kernels  68.6 us (94%)
  between operations  1.8 us (2%)
  local copies, waits for them, and re-layouts  1.35 us (2%)
    pallas_call x1, Pallas kernels, on_device(): pl.pallas_call(functools.partial(kernel, R, emb, width, tracks, frames),...  68.6 us

profile of v5, /device:TPU:6, one launch (start us, length us, event | category | flops | bytes accessed | tf_op | source)
XLA Modules:
  0.0 71.8 jit_solution(5141752468293670863)
XLA Ops:
  0.6 68.6 %shard_map.58 = (f32[3,2,384]{2,1,0:T(2,128)S(1)}, f32[2,128,384]{2,1,0:T(8,128)S(1)}, f32[1,1]{1,0:T(1,128)S(1)}) custom-call(f32[3,2,384]{2,1,0:T(2,128)} %pos.1, f32[2,128,384]{2,1,0:T(8,128)} %emb_in.1, s32[2,384]{1,0:T(2,128)} %vis.1), custom_call_target="tpu_custom_call" | custom-call | tf_op jit(solution)/shard_map/pallas_call | solution.py:513
  69.3 0.6 copy.9
  69.9 0.7 %copy.10 = f32[2,128,384]{2,1,0:T(8,128)} copy(f32[2,128,384]{2,1,0:T(8,128)S(1)} %get-tuple-element.10) | data formatting | bytes 786432
